TPU v7x, 32 devices: a whole 2x2x4 slice. The times are simulated.
32 devices in a mesh: dp: 8 (over z, y), mem: 4 (over x, core).
Axes of the slice: x: 2, y: 2, z: 4, core: 2. Of those that a mesh axis runs over, the one named last changes fastest.
Arguments:
- dec_in: bfloat16 [8, 1024, 1024], P('dp'), may hold values from -6 to 6
- memory: bfloat16 [8, 1024, 1024], P('dp', 'mem'), may hold values from -6 to 6
- dec_len: int32 [8], P('dp'), may hold values from 512 to 1024, as said below
- mem_len: int32 [8], P('dp'), may hold values from 256 to 1024, as said below
- grad_out: bfloat16 [8, 1024, 1024], P('dp'), may hold values from -6 to 6
- self_qkv: bfloat16 [1024, 3072], replicated, may hold values from -0.1875 to 0.1875
- self_out: bfloat16 [1024, 1024], replicated, may hold values from -3 to 3
- cross_q: bfloat16 [1024, 1024], replicated, may hold values from -0.1875 to 0.1875
- cross_kv: bfloat16 [1024, 2048], replicated, may hold values from -0.1875 to 0.1875
- cross_out: bfloat16 [1024, 1024], replicated, may hold values from -3 to 3
- ffn_in: bfloat16 [1024, 4096], replicated, may hold values from -0.1875 to 0.1875
- ffn_out: bfloat16 [4096, 1024], replicated, may hold values from -0.09375 to 0.09375
- proj_bias: float32 [7, 1024], replicated, may hold values from -3 to 3
- ffn_bias: float32 [4096], replicated, may hold values from -3 to 3
- norm_gain: float32 [3, 1024], replicated, may hold values from 0.5 to 1.5
- norm_shift: float32 [3, 1024], replicated, may hold values from -3 to 3
Outputs:
- layer_out: bfloat16 [8, 1024, 1024], P('dp')
- grad_dec: float32 [8, 1024, 1024], P('dp')
- grad_memory: float32 [8, 1024, 1024], P('dp', 'mem')
- grad_self_qkv: float32 [1024, 3072], P('dp')
- grad_self_out: float32 [1024, 1024], P('dp')
- grad_cross_q: float32 [1024, 1024], P('dp')
- grad_cross_kv: float32 [1024, 2048], P('dp')
- grad_cross_out: float32 [1024, 1024], P('dp')
- grad_ffn_in: float32 [1024, 4096], P('dp')
- grad_ffn_out: float32 [4096, 1024], P('dp')
- grad_proj_bias: float32 [7, 1024], replicated
- grad_ffn_bias: float32 [4096], replicated
- grad_norm_gain: float32 [3, 1024], replicated
- grad_norm_shift: float32 [3, 1024], replicated
Inputs may be any that keep to these rules, and one draw needn't show every extreme that they name: `dec_len`: live decoder positions of an item; in every draw some item has all 1024. `mem_len`: valid memory positions of an item, the first ones; in every draw some item has all 1024.
All inputs are finite; a program needn't handle non-finite values.
Results may differ from a plain program's by a relative error of at most 0.023.
Values may be sent and summed in bfloat16 or wider, within the bound.
A program may use at most 448 MiB of HBM per device.

v0:
```python
import jax
import jax.numpy as jnp
from jax import lax
from jax.sharding import PartitionSpec as P

HEAD_DIM = 64
norm_eps = 1e-05
neg_fill = -1e30


def merged(part, axis, combine):
    gathered = jax.tree.map(lambda a: lax.all_gather(a, axis), part)

    def take(source):
        return jax.tree.map(lambda a: lax.dynamic_index_in_dim(a, source, 0, False), gathered)

    return lax.fori_loop(
        1, lax.axis_size(axis), lambda source, state: combine(state, take(source)), take(0)
    )


def product(left_rows, right_rows):
    return jnp.dot(left_rows, right_rows, preferred_element_type=jnp.float32)


def product_tn(left_rows, right_rows):
    return lax.dot_general(
        left_rows, right_rows, (((0,), (0,)), ((), ())), preferred_element_type=jnp.float32
    )


def product_nt(left_rows, right_rows):
    return lax.dot_general(
        left_rows, right_rows, (((1,), (1,)), ((), ())), preferred_element_type=jnp.float32
    )


def split_heads(matrix):
    return matrix.reshape(matrix.shape[0], matrix.shape[1] // HEAD_DIM, HEAD_DIM)


def normalize(hidden, scale_row, shift_row):
    row_mean = jnp.mean(hidden, axis=-1, keepdims=True)
    centered = hidden - row_mean
    variance = jnp.mean(centered * centered, axis=-1, keepdims=True)
    inverse = lax.rsqrt(variance + norm_eps)
    normed = centered * inverse
    return (normed * scale_row + shift_row, normed, inverse)


def norm_back(grad_rows, normed, inverse, scale_row):
    scaled = grad_rows * scale_row
    grad_hidden = inverse * (
        scaled
        - jnp.mean(scaled, axis=-1, keepdims=True)
        - normed * jnp.mean(scaled * normed, axis=-1, keepdims=True)
    )
    return (grad_hidden, jnp.sum(grad_rows * normed, axis=0), jnp.sum(grad_rows, axis=0))


def softmax_rows(scores, allowed, row_max, row_sum):
    masked = jnp.where(allowed, scores, neg_fill)
    return jnp.where(allowed, jnp.exp(masked - row_max), 0.0) / row_sum


def gelu_exact(values):
    return jax.nn.gelu(values, approximate=False)


def merge_stats(first_pair, second_pair):
    larger = jnp.maximum(first_pair[0], second_pair[0])
    return (
        larger,
        first_pair[1] * jnp.exp(first_pair[0] - larger)
        + second_pair[1] * jnp.exp(second_pair[0] - larger),
    )


def column_sum(matrix):
    return jnp.sum(matrix.astype(jnp.float32), axis=0)


def per_device(
    dec_in,
    memory,
    dec_len,
    mem_len,
    grad_out,
    self_qkv,
    self_out,
    cross_q,
    cross_kv,
    cross_out,
    ffn_in,
    ffn_out,
    proj_bias,
    ffn_bias,
    norm_gain,
    norm_shift,
):
    full_rows = dec_in.shape[1]
    model_width = dec_in.shape[2]
    x_rows = dec_in[0]
    mem_rows = memory[0]
    mem_count = mem_rows.shape[0]
    mem_start = lax.axis_index("mem") * mem_count
    zero_bias = jnp.zeros((model_width,), jnp.float32)
    query_pos = jnp.arange(full_rows, dtype=jnp.int32)
    key_pos = jnp.arange(full_rows, dtype=jnp.int32)
    causal = ((key_pos[None, :] <= query_pos[:, None]) & (key_pos[None, :] < dec_len[0]))[None]
    qkv_rows = product(x_rows, self_qkv) + jnp.concatenate([proj_bias[0], zero_bias, proj_bias[1]])
    q_heads = split_heads((qkv_rows[:, :model_width] * 0.125).astype(jnp.bfloat16))
    key_low = qkv_rows[:, model_width : 2 * model_width].astype(jnp.bfloat16)
    value_low = qkv_rows[:, 2 * model_width :].astype(jnp.bfloat16)
    key_all, value_all = (key_low, value_low)
    k_heads = split_heads(key_all)
    v_heads = split_heads(value_all)
    self_scores = jnp.einsum("rhe,che->hrc", q_heads, k_heads, preferred_element_type=jnp.float32)
    self_max = jnp.max(jnp.where(causal, self_scores, neg_fill), axis=-1, keepdims=True)
    self_sum = jnp.sum(
        jnp.where(causal, jnp.exp(jnp.where(causal, self_scores, neg_fill) - self_max), 0.0),
        axis=-1,
        keepdims=True,
    )
    self_weights = softmax_rows(self_scores, causal, self_max, self_sum)
    attended = (
        jnp.einsum(
            "hrc,che->rhe",
            self_weights.astype(jnp.bfloat16),
            v_heads,
            preferred_element_type=jnp.float32,
        )
        .reshape(full_rows, model_width)
        .astype(jnp.bfloat16)
    )
    first_out, first_norm, first_inv = normalize(
        x_rows.astype(jnp.float32) + product(attended, self_out) + proj_bias[2],
        norm_gain[0],
        norm_shift[0],
    )
    first_low = first_out.astype(jnp.bfloat16)
    cq_heads = split_heads(
        ((product(first_low, cross_q) + proj_bias[3]) * 0.125).astype(jnp.bfloat16)
    )
    block_len = mem_rows.shape[0]
    mem_reach = (mem_start + jnp.arange(block_len, dtype=jnp.int32) < mem_len[0])[None, None, :]
    mem_kv = product(mem_rows, cross_kv) + jnp.concatenate([zero_bias, proj_bias[4]])
    kc_heads = split_heads(mem_kv[:, :model_width].astype(jnp.bfloat16))
    vc_heads = split_heads(mem_kv[:, model_width:].astype(jnp.bfloat16))
    cross_scores = jnp.einsum(
        "rhe,che->hrc", cq_heads, kc_heads, preferred_element_type=jnp.float32
    )
    cross_masked = jnp.where(mem_reach, cross_scores, neg_fill)
    local_max = jnp.max(cross_masked, axis=-1)
    local_sum = jnp.sum(
        jnp.where(mem_reach, jnp.exp(cross_masked - local_max[..., None]), 0.0), axis=-1
    )
    cross_max, cross_sum = merged((local_max, local_sum), "mem", merge_stats)
    cross_weights = softmax_rows(
        cross_scores, mem_reach, cross_max[..., None], cross_sum[..., None]
    )
    cross_low = cross_weights.astype(jnp.bfloat16)
    cross_part = jnp.einsum(
        "hrc,che->rhe", cross_low, vc_heads, preferred_element_type=jnp.float32
    ).reshape(full_rows, model_width)
    crossed = lax.psum(cross_part, "mem")
    crossed_low = crossed.astype(jnp.bfloat16)
    second, second_norm, second_inv = normalize(
        first_out + product(crossed_low, cross_out) + proj_bias[5], norm_gain[1], norm_shift[1]
    )
    second_low = second.astype(jnp.bfloat16)
    hidden_pre = product(second_low, ffn_in) + ffn_bias
    activated = gelu_exact(hidden_pre).astype(jnp.bfloat16)
    third_out, third_norm, third_inv = normalize(
        second + product(activated, ffn_out) + proj_bias[6], norm_gain[2], norm_shift[2]
    )
    out_low = third_out.astype(jnp.bfloat16)
    grad_rows_in = grad_out[0]
    cotangent = jnp.where((query_pos < dec_len[0])[:, None], grad_rows_in.astype(jnp.float32), 0.0)
    grad_third, gain_three, shift_three = norm_back(cotangent, third_norm, third_inv, norm_gain[2])
    ffn_grad = grad_third.astype(jnp.bfloat16)
    grad_hidden = product_nt(ffn_grad, ffn_out)
    hidden_grad = jax.vjp(gelu_exact, hidden_pre)[1](grad_hidden)[0].astype(jnp.bfloat16)
    grad_second, gain_two, shift_two = norm_back(
        grad_third + product_nt(hidden_grad, ffn_in), second_norm, second_inv, norm_gain[1]
    )
    cross_grad = grad_second.astype(jnp.bfloat16)
    crossed_grad = split_heads(product_nt(cross_grad, cross_out).astype(jnp.bfloat16))
    grad_vc = jnp.einsum(
        "hrc,rhe->che", cross_low, crossed_grad, preferred_element_type=jnp.float32
    ).reshape(block_len, model_width)
    grad_cw = jnp.einsum("rhe,che->hrc", crossed_grad, vc_heads, preferred_element_type=jnp.float32)
    delta_part = jnp.sum(cross_weights * grad_cw, axis=-1)
    cross_delta = lax.psum(delta_part, "mem")
    cross_ds = (cross_weights * (grad_cw - cross_delta[..., None])).astype(jnp.bfloat16)
    cq_part = jnp.einsum(
        "hrc,che->rhe", cross_ds, kc_heads, preferred_element_type=jnp.float32
    ).reshape(full_rows, model_width)
    cq_total = lax.psum(cq_part, "mem")
    cq_grad = (cq_total * 0.125).astype(jnp.bfloat16)
    grad_kc = jnp.einsum(
        "hrc,rhe->che", cross_ds, cq_heads, preferred_element_type=jnp.float32
    ).reshape(block_len, model_width)
    kv_full = jnp.concatenate([grad_kc, grad_vc], axis=1)
    own_kv = kv_full.astype(jnp.bfloat16)
    grad_memory = product_nt(own_kv, cross_kv)[None]
    grad_first, gain_one, shift_one = norm_back(
        grad_second + product_nt(cq_grad, cross_q), first_norm, first_inv, norm_gain[0]
    )
    self_grad = grad_first.astype(jnp.bfloat16)
    attended_grad = split_heads(product_nt(self_grad, self_out).astype(jnp.bfloat16))
    scores_again = jnp.einsum("rhe,che->hrc", q_heads, k_heads, preferred_element_type=jnp.float32)
    weights_again = softmax_rows(scores_again, causal, self_max, self_sum)
    grad_v = jnp.einsum(
        "hrc,rhe->che",
        weights_again.astype(jnp.bfloat16),
        attended_grad,
        preferred_element_type=jnp.float32,
    ).reshape(full_rows, model_width)
    grad_sw = jnp.einsum("rhe,che->hrc", attended_grad, v_heads, preferred_element_type=jnp.float32)
    self_ds = (
        weights_again * (grad_sw - jnp.sum(weights_again * grad_sw, axis=-1, keepdims=True))
    ).astype(jnp.bfloat16)
    grad_q = (
        jnp.einsum("hrc,che->rhe", self_ds, k_heads, preferred_element_type=jnp.float32).reshape(
            full_rows, model_width
        )
        * 0.125
    )
    grad_k = jnp.einsum(
        "hrc,rhe->che", self_ds, q_heads, preferred_element_type=jnp.float32
    ).reshape(full_rows, model_width)
    grad_k_own, grad_v_own = (grad_k, grad_v)
    qkv_grad = jnp.concatenate([grad_q, grad_k_own, grad_v_own], axis=1).astype(jnp.bfloat16)
    grad_dec_rows = grad_first + product_nt(qkv_grad, self_qkv)
    layer_out = out_low[None]
    grad_dec = grad_dec_rows[None]
    qkv_weight_grad = product_tn(x_rows, qkv_grad)
    self_out_grad = product_tn(attended, self_grad)
    cross_q_grad = product_tn(first_low, cq_grad)
    cross_kv_grad = product_tn(mem_rows, own_kv)
    cross_out_grad = product_tn(crossed_low, cross_grad)
    ffn_in_grad = product_tn(second_low, hidden_grad)
    ffn_out_grad = product_tn(activated, ffn_grad)
    qkv_sums = column_sum(qkv_grad)
    bias_rest = jnp.stack(
        [
            qkv_sums[:model_width],
            qkv_sums[2 * model_width :],
            column_sum(self_grad),
            column_sum(cq_grad),
            column_sum(cross_grad),
            column_sum(ffn_grad),
        ]
    )
    value_bias = column_sum(own_kv[:, model_width:])
    ffn_bias_grad = column_sum(hidden_grad)
    gain_rows = jnp.stack([gain_one, gain_two, gain_three])
    shift_rows = jnp.stack([shift_one, shift_two, shift_three])
    matrices = (
        lax.psum_scatter(qkv_weight_grad, "dp", scatter_dimension=0, tiled=True),
        lax.psum_scatter(self_out_grad, "dp", scatter_dimension=0, tiled=True),
        lax.psum_scatter(cross_q_grad, "dp", scatter_dimension=0, tiled=True),
        lax.psum_scatter(cross_kv_grad, "dp", scatter_dimension=0, tiled=True),
        lax.psum_scatter(cross_out_grad, "dp", scatter_dimension=0, tiled=True),
        lax.psum_scatter(ffn_in_grad, "dp", scatter_dimension=0, tiled=True),
        lax.psum_scatter(ffn_out_grad, "dp", scatter_dimension=0, tiled=True),
    )
    vectors = lax.psum((bias_rest, ffn_bias_grad, gain_rows, shift_rows, value_bias), "dp")
    kv_total, value_total = (
        lax.psum(matrices[3].astype(jnp.bfloat16), "mem").astype(jnp.float32),
        lax.psum(vectors[4].astype(jnp.bfloat16), "mem").astype(jnp.float32),
    )
    matrices = (
        matrices[0],
        matrices[1],
        matrices[2],
        kv_total,
        matrices[4],
        matrices[5],
        matrices[6],
    )
    vectors = (vectors[0], vectors[1], vectors[2], vectors[3], value_total)
    bias_grad = jnp.concatenate([vectors[0][:4], vectors[4][None], vectors[0][4:]], axis=0)
    return (
        layer_out,
        grad_dec,
        grad_memory,
        matrices[0],
        matrices[1],
        matrices[2],
        matrices[3],
        matrices[4],
        matrices[5],
        matrices[6],
        bias_grad,
        vectors[1],
        vectors[2],
        vectors[3],
    )


def solution(mesh):
    in_specs = (
        P("dp", None, None),
        P("dp", "mem", None),
        P("dp"),
        P("dp"),
        P("dp", None, None),
        P(),
        P(),
        P(),
        P(),
        P(),
        P(),
        P(),
        P(),
        P(),
        P(),
        P(),
    )
    out_specs = (
        P("dp", None, None),
        P("dp", None, None),
        P("dp", "mem", None),
        P("dp", None),
        P("dp", None),
        P("dp", None),
        P("dp", None),
        P("dp", None),
        P("dp", None),
        P("dp", None),
        P(),
        P(),
        P(),
        P(),
    )
    return jax.shard_map(
        per_device, mesh=mesh, in_specs=in_specs, out_specs=out_specs, check_vma=False
    )
```

profile of v0, /device:TPU:0, one launch (start us, length us, event | category | flops | bytes accessed | tf_op | source)
XLA Modules:
  0.0 1810.6 jit_solution(15955320089730400923)
XLA Ops:
  27.2 12.1 fusion.80
  57.7 35.8 %fusion.81 = (f32[16,1024]{1,0:T(8,128)S(1)}, f32[16,1024,1024]{1,2,0:T(8,128)}) fusion(pred[1024,1024]{0,1:T(8,128)(4,1)S(1)} %fusion.35, bf16[1024,16,64]{0,2,1:T(8,128)(2,1)} %bitcast.166, bf16[1024,16,64]{0,2,1:T(8,128)(2,1)} %bitcast.171), kind=kOutput, calls=%fused_computation.155 | convolution fusion | flops 2214593536 | bytes 72417280 | tf_op jit(solution)/shard_map/sub | solution.py:63
  93.5 24.3 %fusion.42 = bf16[16,64,1024]{2,1,0:T(8,128)(2,1)} fusion(bf16[1024,16,64]{0,2,1:T(8,128)(2,1)} %bitcast.181, f32[16,1024,1024]{1,2,0:T(8,128)} %get-tuple-element.239, f32[16,1024]{1,0:T(8,128)S(1)} %get-tuple-element.238), kind=kOutput, calls=%fused_computation.103 | convolution fusion | flops 2182086656 | bytes 71368704 | tf_op jit(solution)/shard_map/hrc,che->rhe/dot_general | solution.py:127
  117.9 4.3 fusion.82
  132.1 8.9 select_reduce_fusion.2
  141.0 7.2 all-gather
  148.2 9.6 select_reduce_fusion.1
  157.8 5.9 all-gather.1
  163.9 10.4 fusion.33
  174.4 77.8 %all-reduce.13 = bf16[1024,1024]{0,1:T(8,128)(2,1)} all-reduce(f32[1024,1024]{0,1:T(8,128)} %bitcast.178), channel_id=1, replica_groups=mesh['dp'=8,'mem'=4] {'mem'}, use_global_device_ids=true, to_apply=%region_8.9 | all-reduce | flops 1048576 | bytes 6291456 | tf_op jit(solution)/shard_map/psum | solution.py:166
  252.2 6.5 fusion.83
  260.7 47.8 %multiply_convert_fusion.2 = (bf16[1024,4096]{1,0:T(8,128)(2,1)}, f32[1024,4096]{1,0:T(8,128)}, f32[1024,4096]{1,0:T(8,128)}) fusion(f32[4096]{0:T(1024)S(1)} %copy-done.76, bf16[1024,4096]{1,0:T(8,128)(2,1)} %param.28, bf16[1024,1024]{0,1:T(8,128)(2,1)S(1)} %fusion.69.clone.4), kind=kOutput, calls=%fused_computation.20 | convolution fusion | flops 8866758656 | bytes 52445184 | tf_op jit(solution)/shard_map/dot_general | solution.py:23
  308.5 16.8 fusion.84
  331.8 4.3 convert_reduce_fusion.2
  336.0 24.5 %convert_reduce_fusion = (f32[4096]{0:T(1024)}, bf16[1024,4096]{1,0:T(8,128)(2,1)}) fusion(f32[1024,4096]{1,0:T(8,128)} %get-tuple-element.215, f32[1024,4096]{1,0:T(8,128)} %get-tuple-element.246, f32[4096]{0:T(1024)S(1)} %copy-done.76, bf16[1024,1024]{0,1:T(8,128)(2,1)} %get-tuple-element.209, bf16[4096,1024]{1,0:T(8,128)(2,1)} %param.29), kind=kOutput, calls=%fused_computation.16 | convolution fusion | flops 8661233664 | bytes 52461568 | tf_op jit(solution)/shard_map/dot_general | solution.py:33
  360.5 18.5 %multiply_reduce_fusion.2 = (f32[1024]{0:T(1024)}, f32[1024]{0:T(1024)S(1)}, f32[1024]{0:T(1024)S(1)}, f32[1024]{0:T(1024)}, f32[1024,1024]{0,1:T(8,128)S(1)}) fusion(f32[1024,1024]{0,1:T(8,128)S(1)} %copy-done.4, f32[1024]{0:T(1024)S(1)} %add_rsqrt_fusion.1, f32[1024]{0:T(1024)S(1)} %broadcast_multiply_fusion.7, f32[1024]{0:T(1024)S(1)} %bitcast.194, ...), kind=kOutput, calls=%fused_computation.60 | convolution fusion | flops 8609853440 | bytes 31507456 | tf_op jit(solution)/shard_map/dot_general | solution.py:33
  383.5 14.6 multiply_reduce_fusion.1
  398.1 31.9 %all-reduce.8.cloned.1.call-done = f32[16,1024]{1,0:T(8,128)} async-done(((f32[16,1024]{1,0:T(8,128)}), f32[16,1024]{1,0:T(8,128)}) %all-reduce.8.cloned.1.call-update) | async-done | bytes 65552 | tf_op jit(solution)/shard_map/psum | solution.py:194
  430.0 12.4 multiply_convert_fusion.1
  446.8 5.3 copy.76
  452.3 9.6 fusion.48
  461.9 6.3 convolution_convert_fusion.3
  469.1 4.5 convolution_bitcast_fusion.1
  473.6 64.2 %all-reduce.10.cloned.1.call-done = f32[1024,1024]{1,0:T(8,128)} async-done(((f32[1024,1024]{1,0:T(8,128)}), f32[1024,1024]{1,0:T(8,128)}) %all-reduce.10.cloned.1.call-update) | async-done | bytes 4194320 | tf_op jit(solution)/shard_map/psum | solution.py:199
  537.9 8.5 multiply_reduce_fusion.3
  551.6 43.5 %multiply_reduce_fusion = (f32[16,1024]{1,0:T(8,128)S(1)}, f32[16,1024,1024]{1,2,0:T(8,128)}) fusion(f32[16,1024,1024]{1,2,0:T(8,128)} %get-tuple-element.239, f32[16,1024]{1,0:T(8,128)S(1)} %copy-done.33, bf16[1024,16,64]{0,2,1:T(8,128)(2,1)S(1)} %bitcast.235, bf16[1024,16,64]{0,2,1:T(8,128)(2,1)S(1)} %bitcast.182), kind=kOutput, calls=%fused_computation.7 | convolution fusion | flops 2197798912 | bytes 138543104 | tf_op jit(solution)/shard_map/rhe,che->hrc/dot_general | solution.py:220
  595.1 54.7 %multiply_convert_fusion = bf16[16,1024,1024]{1,2,0:T(8,128)(2,1)} fusion(f32[16,1024,1024]{1,2,0:T(8,128)} %get-tuple-element.254, f32[16,1024]{1,0:T(8,128)S(1)} %get-tuple-element.253, f32[16,1024,1024]{1,2,0:T(8,128)} %get-tuple-element.239, f32[16,1024]{1,0:T(8,128)S(1)} %copy-done.33), kind=kLoop, calls=%fused_computation.6 | loop fusion | flops 67108864 | bytes 167903232 | tf_op jit(solution)/shard_map/convert_element_type | solution.py:223
  649.8 17.3 convolution_convert_fusion
  667.2 18.7 %multiply_convert_fusion.3 = bf16[16,64,1024]{2,1,0:T(8,128)(2,1)} fusion(bf16[1024,16,64]{0,2,1:T(8,128)(2,1)} %bitcast.172, bf16[16,1024,1024]{1,2,0:T(8,128)(2,1)} %multiply_convert_fusion), kind=kOutput, calls=%fused_computation.67 | convolution fusion | flops 2149580800 | bytes 37748736 | tf_op jit(solution)/shard_map/hrc,che->rhe/dot_general | solution.py:225
  685.9 25.3 %fusion.45 = bf16[16,64,1024]{2,1,0:T(8,128)(2,1)} fusion(bf16[1024,16,64]{0,2,1:T(8,128)(2,1)} %bitcast.236, f32[16,1024,1024]{1,2,0:T(8,128)} %get-tuple-element.239, f32[16,1024]{1,0:T(8,128)S(1)} %copy-done.33), kind=kOutput, calls=%fused_computation.104 | convolution fusion | flops 2182086656 | bytes 71368704 | tf_op jit(solution)/shard_map/hrc,rhe->che/dot_general | solution.py:214
  713.3 13.7 convolution_bitcast_fusion
  727.3 7.3 fusion.51
  735.3 7.9 fusion.65
  743.3 7.1 fusion.59
  751.1 16.6 fusion.66
  768.1 16.3 fusion.86
  789.6 4.6 convolution_bitcast_fusion.2
  794.4 4.6 convert_reduce_fusion.1
  799.5 41.7 %all-reduce.14 = (f32[6,1024]{1,0:T(8,128)S(1)}, bf16[1024]{0:T(1024)(128)(2,1)S(1)}, f32[4096]{0:T(1024)}, f32[3,1024]{1,0:T(4,128)}, f32[3,1024]{1,0:T(4,128)}) all-reduce(f32[6,1024]{1,0:T(8,128)S(1)} %stack.51, f32[1024]{0:T(1024)S(1)} %convert_reduce_fusion.6, f32[4096]{0:T(1024)S(1)} %copy-done.58, ...), channel_id=1, replica_groups=mesh['dp'=8,'mem'=4] {'dp'}, use_global_device_ids=true, to_apply=%region_36.37 | all-reduce | flops 17408 | bytes 137216 | tf_op jit(solution)/shard_map/psum | solution.py:269
  841.2 12.4 add_bitcast_fusion
  853.6 5.5 copy.85
  859.2 6.1 psum.76
  868.1 91.6 %reduce-scatter.8.cloned.1.call-done = f32[128,3072]{0,1:T(8,128)} async-done(((f32[1024,3072]{0,1:T(8,128)}), f32[128,3072]{0,1:T(8,128)}) %reduce-scatter.8.cloned.1.call-update) | async-done | bytes 1572880 | tf_op jit(solution)/shard_map/reduce_scatter | solution.py:261
  962.7 88.5 %reduce-scatter.16.cloned.1.call-done = f32[128,1024]{1,0:T(8,128)} async-done(((f32[1024,1024]{1,0:T(8,128)}), f32[128,1024]{1,0:T(8,128)}) %reduce-scatter.16.cloned.1.call-update) | async-done | bytes 524304 | tf_op jit(solution)/shard_map/reduce_scatter | solution.py:265
  1051.2 92.2 %reduce-scatter.12.cloned.1.call-done = f32[128,1024]{1,0:T(8,128)} async-done(((f32[1024,1024]{1,0:T(8,128)}), f32[128,1024]{1,0:T(8,128)}) %reduce-scatter.12.cloned.1.call-update) | async-done | bytes 524304 | tf_op jit(solution)/shard_map/reduce_scatter | solution.py:263
  1143.4 92.2 %reduce-scatter.10.cloned.1.call-done = f32[128,1024]{1,0:T(8,128)} async-done(((f32[1024,1024]{1,0:T(8,128)}), f32[128,1024]{1,0:T(8,128)}) %reduce-scatter.10.cloned.1.call-update) | async-done | bytes 524304 | tf_op jit(solution)/shard_map/reduce_scatter | solution.py:262
  1235.6 284.2 %reduce-scatter.18.cloned.1.call-done = f32[128,4096]{1,0:T(8,128)} async-done(((f32[1024,4096]{1,0:T(8,128)}), f32[128,4096]{1,0:T(8,128)}) %reduce-scatter.18.cloned.1.call-update) | async-done | bytes 2097168 | tf_op jit(solution)/shard_map/reduce_scatter | solution.py:266
  1519.8 283.5 %reduce-scatter.20.cloned.1.call-done = f32[512,1024]{1,0:T(8,128)} async-done(((f32[4096,1024]{1,0:T(8,128)}), f32[512,1024]{1,0:T(8,128)}) %reduce-scatter.20.cloned.1.call-update) | async-done | bytes 2097168 | tf_op jit(solution)/shard_map/reduce_scatter | solution.py:267
  (244 shorter events, 86.5 us)
Async XLA Ops:
  7.2 116.9 %copy-start = (bf16[1024,1024]{1,0:T(8,128)(2,1)S(1)}, bf16[1024,1024]{1,0:T(8,128)(2,1)}, u32[]{:S(2)}) copy-start(bf16[1024,1024]{1,0:T(8,128)(2,1)} %param.25) | copy-start | bytes 6291460
  7.2 422.8 %all-reduce.8.cloned.1.call-start = ((), (), s32[]{:S(2)}) async-start(), calls=%async_computation.7 | async-start | bytes 131072 | tf_op jit(solution)/shard_map/psum | solution.py:194
  8.7 10.3 copy-start.59
  93.5 24.3 %copy-start.32 = (f32[16,1024]{1,0:T(8,128)}, f32[16,1024]{1,0:T(8,128)S(1)}, u32[]{:S(2)}) copy-start(f32[16,1024]{1,0:T(8,128)S(1)} %get-tuple-element.238) | copy-start | bytes 196612
  93.5 24.3 %copy-start.26 = (bf16[1,1024,1024]{1,2,0:T(8,128)(2,1)S(1)}, bf16[1,1024,1024]{1,2,0:T(8,128)(2,1)}, u32[]{:S(2)}) copy-start(bf16[1,1024,1024]{1,2,0:T(8,128)(2,1)} %copy.62) | copy-start | bytes 6291460
  93.5 24.3 %copy-start.66 = (f32[1,1024]{1,0:T(1,128)S(1)}, f32[1,1024]{1,0:T(1,128)}, u32[]{:S(2)}) copy-start(f32[1,1024]{1,0:T(1,128)} %get-tuple-element.224) | copy-start | bytes 12292
  93.5 24.3 %copy-start.74 = (bf16[1024,1024]{1,0:T(8,128)(2,1)S(1)}, bf16[1024,1024]{1,0:T(8,128)(2,1)}, u32[]{:S(2)}) copy-start(bf16[1024,1024]{1,0:T(8,128)(2,1)} %param.24) | copy-start | bytes 6291460
  122.2 129.9 %copy-start.41 = (f32[1024]{0:T(1024)}, f32[1024]{0:T(1024)S(1)}, u32[]{:S(2)}) copy-start(f32[1024]{0:T(1024)S(1)} %broadcast_multiply_fusion.8) | copy-start | bytes 12292
  122.7 129.4 %copy-start.49 = (f32[1024]{0:T(1024)}, f32[1024]{0:T(1024)S(1)}, u32[]{:S(2)}) copy-start(f32[1024]{0:T(1024)S(1)} %add_rsqrt_fusion.2) | copy-start | bytes 12292
  132.1 31.8 %copy-start.61 = (pred[256]{0:T(512)(128)(4,1)}, pred[256]{0:T(512)(128)(4,1)S(1)}, u32[]{:S(2)}) copy-start(pred[256]{0:T(512)(128)(4,1)S(1)} %add_compare_fusion) | copy-start | bytes 772
  148.2 15.7 copy-start.30
  163.9 10.5 copy-start.18
  163.9 10.5 copy-start.20
  174.4 77.8 %copy-start.64 = (f32[1,1024]{1,0:T(1,128)S(1)}, f32[1,1024]{1,0:T(1,128)}, u32[]{:S(2)}) copy-start(f32[1,1024]{1,0:T(1,128)} %get-tuple-element.227) | copy-start | bytes 12292
  258.7 120.2 %copy-start.34 = (f32[1024]{0:T(1024)}, f32[1024]{0:T(1024)S(1)}, u32[]{:S(2)}) copy-start(f32[1024]{0:T(1024)S(1)} %broadcast_multiply_fusion.7) | copy-start | bytes 12292
  259.2 119.7 %copy-start.36 = (f32[1024]{0:T(1024)}, f32[1024]{0:T(1024)S(1)}, u32[]{:S(2)}) copy-start(f32[1024]{0:T(1024)S(1)} %add_rsqrt_fusion.1) | copy-start | bytes 12292
  260.7 47.8 %copy-start.63 = (f32[1,1024]{1,0:T(1,128)S(1)}, f32[1,1024]{1,0:T(1,128)}, u32[]{:S(2)}) copy-start(f32[1,1024]{1,0:T(1,128)} %get-tuple-element.221) | copy-start | bytes 12292
  308.5 19.7 %copy-start.6 = (bf16[1,1024,1024]{1,2,0:T(8,128)(2,1)S(1)}, bf16[1,1024,1024]{1,2,0:T(8,128)(2,1)}, u32[]{:S(2)}) copy-start(bf16[1,1024,1024]{1,2,0:T(8,128)(2,1)} %copy.73) | copy-start | bytes 6291460
  336.0 24.5 %copy-start.4 = (f32[1024,1024]{0,1:T(8,128)S(1)}, f32[1024,1024]{0,1:T(8,128)}, u32[]{:S(2)}) copy-start(f32[1024,1024]{0,1:T(8,128)} %copy-done.3) | copy-start | bytes 12582916
  383.4 14.6 copy-start.77
  398.1 139.8 %all-reduce.10.cloned.1.call-start = ((), (), s32[]{:S(2)}) async-start(), calls=%async_computation.8 | async-start | bytes 8388608 | tf_op jit(solution)/shard_map/psum | solution.py:199
  430.0 12.4 copy-start.14
  452.2 259.0 %reduce-scatter.14.cloned.1.call-start = ((), (), s32[]{:S(2)}) async-start(), calls=%async_computation.12 | async-start | bytes 9437184 | tf_op jit(solution)/shard_map/reduce_scatter | solution.py:264
  452.3 9.6 copy-start.7
  461.9 6.4 copy-start.22
  461.9 7.1 copy-start.29
  473.5 64.3 %copy-start.42 = (f32[1024]{0:T(1024)S(1)}, f32[1024]{0:T(1024)}, u32[]{:S(2)}) copy-start(f32[1024]{0:T(1024)} %copy-done.41) | copy-start | bytes 12292
  473.6 64.3 %copy-start.50 = (f32[1024]{0:T(1024)S(1)}, f32[1024]{0:T(1024)}, u32[]{:S(2)}) copy-start(f32[1024]{0:T(1024)} %copy-done.49) | copy-start | bytes 12292
  473.6 64.3 %copy-start.55 = (f32[1,1024]{1,0:T(1,128)S(1)}, f32[1,1024]{1,0:T(1,128)}, u32[]{:S(2)}) copy-start(f32[1,1024]{1,0:T(1,128)} %get-tuple-element.229) | copy-start | bytes 12292
  473.6 392.3 %all-reduce.12.cloned.1.call-start = ((), (), s32[]{:S(2)}) async-start(), calls=%async_computation.13 | async-start | bytes 1048576 | tf_op jit(solution)/shard_map/psum | solution.py:271
  537.9 8.5 copy-start.9
  550.8 44.3 %copy-start.78 = (bf16[1024,1024]{0,1:T(8,128)(2,1)}, bf16[1024,1024]{0,1:T(8,128)(2,1)S(1)}, u32[]{:S(2)}) copy-start(bf16[1024,1024]{0,1:T(8,128)(2,1)S(1)} %convolution_convert_fusion.1) | copy-start | bytes 6291460
  595.1 54.7 %copy-start.10 = (bf16[1024,1024]{0,1:T(8,128)(2,1)S(1)}, bf16[1024,1024]{0,1:T(8,128)(2,1)}, u32[]{:S(2)}) copy-start(bf16[1024,1024]{0,1:T(8,128)(2,1)} %copy.64) | copy-start | bytes 6291460
  685.9 27.4 %copy-start.11 = (bf16[16,64,1024]{2,1,0:T(8,128)(2,1)S(1)}, bf16[16,64,1024]{2,1,0:T(8,128)(2,1)}, u32[]{:S(2)}) copy-start(bf16[16,64,1024]{2,1,0:T(8,128)(2,1)} %convolution_convert_fusion) | copy-start | bytes 6291460
  713.3 246.4 %reduce-scatter.8.cloned.1.call-start = ((), (), s32[]{:S(2)}) async-start(), calls=%async_computation.9 | async-start | bytes 14155776 | tf_op jit(solution)/shard_map/reduce_scatter | solution.py:261
  727.0 324.2 %reduce-scatter.16.cloned.1.call-start = ((), (), s32[]{:S(2)}) async-start(), calls=%async_computation.14 | async-start | bytes 4718592 | tf_op jit(solution)/shard_map/reduce_scatter | solution.py:265
  734.6 408.8 %reduce-scatter.12.cloned.1.call-start = ((), (), s32[]{:S(2)}) async-start(), calls=%async_computation.11 | async-start | bytes 4718592 | tf_op jit(solution)/shard_map/reduce_scatter | solution.py:263
  743.3 492.4 %reduce-scatter.10.cloned.1.call-start = ((), (), s32[]{:S(2)}) async-start(), calls=%async_computation.10 | async-start | bytes 4718592 | tf_op jit(solution)/shard_map/reduce_scatter | solution.py:262
  750.5 769.3 %reduce-scatter.18.cloned.1.call-start = ((), (), s32[]{:S(2)}) async-start(), calls=%async_computation.15 | async-start | bytes 18874368 | tf_op jit(solution)/shard_map/reduce_scatter | solution.py:266
  767.8 1035.5 %reduce-scatter.20.cloned.1.call-start = ((), (), s32[]{:S(2)}) async-start(), calls=%async_computation.16 | async-start | bytes 18874368 | tf_op jit(solution)/shard_map/reduce_scatter | solution.py:267
  794.3 5.1 copy-start.48
  794.3 5.1 copy-start.68
  794.3 5.1 copy-start.70
  794.3 5.1 copy-start.47
  794.3 5.1 copy-start.67
  794.3 5.1 copy-start.69
  794.3 5.1 copy-start.58
  853.6 949.7 %copy-start.1 = (bf16[1024,1024]{1,0:T(8,128)(2,1)S(1)}, bf16[1024,1024]{1,0:T(8,128)(2,1)}, u32[]{:S(2)}) copy-start(bf16[1024,1024]{1,0:T(8,128)(2,1)} %param.25) | copy-start | bytes 6291460
  (41 other events, 100.6 us)
Sparse Core Ops, SparseCore 0:
  398.2 31.7 all-reduce.7
  452.3 85.4 all-reduce.9
  541.5 147.9 reduce-scatter.13
  713.4 33.2 all-reduce.11
  750.1 209.5 reduce-scatter.7
  963.8 87.3 reduce-scatter.15
  1055.4 87.9 reduce-scatter.11
  1147.6 87.9 reduce-scatter.9
  1240.0 279.7 reduce-scatter.17
  1524.0 279.2 reduce-scatter.19
where the time goes:
time: 1820 us; the launch traced here: 1810 us
  waiting for transfers between devices  1030 us (57%)
  matrix products  461 us (25%)
  blocking collectives  139 us (8%)
  other arithmetic  105 us (6%)
  local copies, waits for them, and re-layouts  60.3 us (3%)
    reduce_scatter x1, waiting for transfers between devices, per_device(): lax.psum_scatter(ffn_in_grad, 'dp', scatter_dimension=0, tiled=True)  284 us
    reduce_scatter x1, waiting for transfers between devices, per_device(): lax.psum_scatter(ffn_out_grad, 'dp', scatter_dimension=0, tiled=True)  284 us
    dot_general x7, matrix products, product(): return jnp.dot(left_rows, right_rows, preferred_element_type=jnp.float32)  95.2 us
    reduce_scatter x1, waiting for transfers between devices, per_device(): lax.psum_scatter(self_out_grad, 'dp', scatter_dimension=0, tiled=True)  92.2 us
    reduce_scatter x1, waiting for transfers between devices, per_device(): lax.psum_scatter(cross_q_grad, 'dp', scatter_dimension=0, tiled=True)  92.2 us
    reduce_scatter x1, waiting for transfers between devices, per_device(): lax.psum_scatter(qkv_weight_grad, 'dp', scatter_dimension=0, tiled=True)  91.6 us
    reduce_scatter x1, waiting for transfers between devices, per_device(): lax.psum_scatter(cross_out_grad, 'dp', scatter_dimension=0, tiled=True)  88.5 us
    psum x1, blocking collectives, per_device(): crossed = lax.psum(cross_part, 'mem')  77.8 us
  transfers between devices with their start and end apart: 10, of which 8 were waited for; matrix products, arithmetic and copies ran while one was open for 17% of the time, Pallas kernels for 0%

commit v1 on v0

--- a/solution.py
+++ b/solution.py
@@ -6,6 +6,14 @@
 HEAD_DIM = 64
 norm_eps = 1e-05
 neg_fill = -1e30
+
+
+def doubling_sum(x, name):
+    n_dev, result = (lax.axis_size(name), x)
+    for far in [1 << k for k in range(n_dev.bit_length() - 1)]:
+        route = [(i, i ^ far) for i in range(n_dev)]
+        result = result + lax.ppermute(result, name, route)
+    return result
 
 
 def merged(part, axis, combine):
@@ -163,7 +171,7 @@
     cross_part = jnp.einsum(
         "hrc,che->rhe", cross_low, vc_heads, preferred_element_type=jnp.float32
     ).reshape(full_rows, model_width)
-    crossed = lax.psum(cross_part, "mem")
+    crossed = doubling_sum(cross_part, "mem")
     crossed_low = crossed.astype(jnp.bfloat16)
     second, second_norm, second_inv = normalize(
         first_out + product(crossed_low, cross_out) + proj_bias[5], norm_gain[1], norm_shift[1]

time: 1820 us -> 1840 us (1.011)
  waiting for transfers between devices: 1030 us -> 1120 us
  blocking collectives: 139 us -> 61 us
    ppermute x0 -> x2, waiting for transfers between devices: none -> 94.5 us  [doubling_sum(): result = result + lax.ppermute(result, name, route)]
    psum x1 -> x0, blocking collectives: 77.8 us -> none  [per_device(): crossed = lax.psum(cross_part, 'mem')]
  transfers between devices with their start and end apart: 10 -> 12, of which waited for: 8 -> 10; matrix products, arithmetic and copies ran while one was open for 17% -> 17% of each run, Pallas kernels for 0% -> 0%
where the time goes in v1:
time: 1840 us; the launch traced here: 1830 us
  waiting for transfers between devices  1120 us (61%)
  matrix products  454 us (25%)
  other arithmetic  112 us (6%)
  blocking collectives  61 us (3%)
  local copies, waits for them, and re-layouts  60.3 us (3%)
    reduce_scatter x1, waiting for transfers between devices, per_device(): lax.psum_scatter(ffn_in_grad, 'dp', scatter_dimension=0, tiled=True)  284 us
    reduce_scatter x1, waiting for transfers between devices, per_device(): lax.psum_scatter(ffn_out_grad, 'dp', scatter_dimension=0, tiled=True)  284 us
    ppermute x2, waiting for transfers between devices, doubling_sum(): result = result + lax.ppermute(result, name, route)  94.5 us
    reduce_scatter x1, waiting for transfers between devices, per_device(): lax.psum_scatter(cross_q_grad, 'dp', scatter_dimension=0, tiled=True)  92.2 us
    reduce_scatter x1, waiting for transfers between devices, per_device(): lax.psum_scatter(self_out_grad, 'dp', scatter_dimension=0, tiled=True)  92.2 us
    reduce_scatter x1, waiting for transfers between devices, per_device(): lax.psum_scatter(qkv_weight_grad, 'dp', scatter_dimension=0, tiled=True)  91.6 us
    dot_general x7, matrix products, product(): return jnp.dot(left_rows, right_rows, preferred_element_type=jnp.float32)  90.6 us
    reduce_scatter x1, waiting for transfers between devices, per_device(): lax.psum_scatter(cross_out_grad, 'dp', scatter_dimension=0, tiled=True)  88.5 us
  transfers between devices with their start and end apart: 12, of which 10 were waited for; matrix products, arithmetic and copies ran while one was open for 17% of the time, Pallas kernels for 0%

profile of v1, /device:TPU:0, one launch (start us, length us, event | category | flops | bytes accessed | tf_op | source)
XLA Modules:
  0.0 1831.1 jit_solution(13103761637117372332)
XLA Ops:
  23.3 12.1 fusion.78
  53.7 35.8 %fusion.79 = (f32[16,1024]{1,0:T(8,128)S(1)}, f32[16,1024,1024]{1,2,0:T(8,128)}) fusion(pred[1024,1024]{0,1:T(8,128)(4,1)S(1)} %fusion.35, bf16[1024,16,64]{0,2,1:T(8,128)(2,1)} %bitcast.167, bf16[1024,16,64]{0,2,1:T(8,128)(2,1)} %bitcast.172), kind=kOutput, calls=%fused_computation.155 | convolution fusion | flops 2214593536 | bytes 72417280 | tf_op jit(solution)/shard_map/sub | solution.py:71
  89.6 24.3 %fusion.42 = bf16[16,64,1024]{2,1,0:T(8,128)(2,1)} fusion(bf16[1024,16,64]{0,2,1:T(8,128)(2,1)} %bitcast.182, f32[16,1024,1024]{1,2,0:T(8,128)} %get-tuple-element.239, f32[16,1024]{1,0:T(8,128)S(1)} %get-tuple-element.238), kind=kOutput, calls=%fused_computation.104 | convolution fusion | flops 2182086656 | bytes 71368704 | tf_op jit(solution)/shard_map/hrc,che->rhe/dot_general | solution.py:135
  113.9 4.3 fusion.80
  128.2 8.9 select_reduce_fusion.2
  137.0 7.2 all-gather
  144.3 9.6 select_reduce_fusion.1
  153.8 6.1 all-gather.1
  160.2 8.1 fusion.33
  168.7 6.8 collective-permute-done
  184.0 87.7 %collective-permute-done.1 = f32[1024,1024]{0,1:T(8,128)} collective-permute-done((f32[1024,1024]{0,1:T(8,128)}, f32[1024,1024]{0,1:T(8,128)}, u32[]{:S(2)}, u32[]{:S(2)}) %collective-permute-start.1) | collective-permute-done | bytes 4194336 | tf_op jit(solution)/shard_map/ppermute | solution.py:15
  271.6 4.3 add_convert_fusion.2
  281.4 46.4 %multiply_convert_fusion.2 = (bf16[1024,4096]{1,0:T(8,128)(2,1)}, f32[1024,4096]{1,0:T(8,128)}, f32[1024,4096]{1,0:T(8,128)}) fusion(f32[4096]{0:T(1024)S(1)} %copy-done.79, bf16[1024,4096]{1,0:T(8,128)(2,1)S(1)} %bitcast.233, bf16[1024,1024]{0,1:T(8,128)(2,1)S(1)} %fusion.67.clone.4), kind=kOutput, calls=%fused_computation.20 | convolution fusion | flops 8866758656 | bytes 52445184 | tf_op jit(solution)/shard_map/dot_general | solution.py:31
  327.8 16.9 fusion.82
  355.3 24.5 %convert_reduce_fusion = (f32[4096]{0:T(1024)}, bf16[1024,4096]{1,0:T(8,128)(2,1)}) fusion(f32[1024,4096]{1,0:T(8,128)} %get-tuple-element.215, f32[1024,4096]{1,0:T(8,128)} %get-tuple-element.246, f32[4096]{0:T(1024)S(1)} %copy-done.79, bf16[1024,1024]{0,1:T(8,128)(2,1)} %get-tuple-element.209, bf16[4096,1024]{1,0:T(8,128)(2,1)} %param.29), kind=kOutput, calls=%fused_computation.16 | convolution fusion | flops 8661233664 | bytes 52461568 | tf_op jit(solution)/shard_map/dot_general | solution.py:41
  379.8 18.5 %multiply_reduce_fusion.2 = (f32[1024]{0:T(1024)}, f32[1024]{0:T(1024)S(1)}, f32[1024]{0:T(1024)S(1)}, f32[1024]{0:T(1024)}, f32[1024,1024]{0,1:T(8,128)S(1)}) fusion(f32[1024,1024]{0,1:T(8,128)S(1)} %copy-done.4, f32[1024]{0:T(1024)S(1)} %add_rsqrt_fusion.1, f32[1024]{0:T(1024)S(1)} %broadcast_multiply_fusion.7, f32[1024]{0:T(1024)S(1)} %bitcast.195, ...), kind=kOutput, calls=%fused_computation.60 | convolution fusion | flops 8609853440 | bytes 31507456 | tf_op jit(solution)/shard_map/dot_general | solution.py:41
  402.8 14.6 multiply_reduce_fusion.1
  417.4 32.9 %all-reduce.7.cloned.1.call-done = f32[16,1024]{1,0:T(8,128)} async-done(((f32[16,1024]{1,0:T(8,128)}), f32[16,1024]{1,0:T(8,128)}) %all-reduce.7.cloned.1.call-update) | async-done | bytes 65552 | tf_op jit(solution)/shard_map/psum | solution.py:202
  450.3 12.4 multiply_convert_fusion.1
  467.1 5.4 copy.76
  472.6 9.6 fusion.48
  482.3 6.3 convolution_convert_fusion.3
  489.4 4.5 convolution_bitcast_fusion.1
  493.9 64.2 %all-reduce.9.cloned.1.call-done = f32[1024,1024]{1,0:T(8,128)} async-done(((f32[1024,1024]{1,0:T(8,128)}), f32[1024,1024]{1,0:T(8,128)}) %all-reduce.9.cloned.1.call-update) | async-done | bytes 4194320 | tf_op jit(solution)/shard_map/psum | solution.py:207
  558.2 8.5 multiply_reduce_fusion.3
  571.9 43.5 %multiply_reduce_fusion = (f32[16,1024]{1,0:T(8,128)S(1)}, f32[16,1024,1024]{1,2,0:T(8,128)}) fusion(f32[16,1024,1024]{1,2,0:T(8,128)} %get-tuple-element.239, f32[16,1024]{1,0:T(8,128)S(1)} %copy-done.35, bf16[1024,16,64]{0,2,1:T(8,128)(2,1)S(1)} %bitcast.238, bf16[1024,16,64]{0,2,1:T(8,128)(2,1)S(1)} %bitcast.183), kind=kOutput, calls=%fused_computation.7 | convolution fusion | flops 2197798912 | bytes 138543104 | tf_op jit(solution)/shard_map/rhe,che->hrc/dot_general | solution.py:228
  615.4 54.7 %multiply_convert_fusion = bf16[16,1024,1024]{1,2,0:T(8,128)(2,1)} fusion(f32[16,1024,1024]{1,2,0:T(8,128)} %get-tuple-element.254, f32[16,1024]{1,0:T(8,128)S(1)} %get-tuple-element.253, f32[16,1024,1024]{1,2,0:T(8,128)} %get-tuple-element.239, f32[16,1024]{1,0:T(8,128)S(1)} %copy-done.35), kind=kLoop, calls=%fused_computation.6 | loop fusion | flops 67108864 | bytes 167903232 | tf_op jit(solution)/shard_map/convert_element_type | solution.py:231
  670.1 17.3 convolution_convert_fusion
  687.5 18.8 %multiply_convert_fusion.3 = bf16[16,64,1024]{2,1,0:T(8,128)(2,1)} fusion(bf16[1024,16,64]{0,2,1:T(8,128)(2,1)} %bitcast.173, bf16[16,1024,1024]{1,2,0:T(8,128)(2,1)} %multiply_convert_fusion), kind=kOutput, calls=%fused_computation.67 | convolution fusion | flops 2149580800 | bytes 37748736 | tf_op jit(solution)/shard_map/hrc,che->rhe/dot_general | solution.py:233
  706.2 25.3 %fusion.45 = bf16[16,64,1024]{2,1,0:T(8,128)(2,1)} fusion(bf16[1024,16,64]{0,2,1:T(8,128)(2,1)} %bitcast.239, f32[16,1024,1024]{1,2,0:T(8,128)} %get-tuple-element.239, f32[16,1024]{1,0:T(8,128)S(1)} %copy-done.35), kind=kOutput, calls=%fused_computation.105 | convolution fusion | flops 2182086656 | bytes 71368704 | tf_op jit(solution)/shard_map/hrc,rhe->che/dot_general | solution.py:222
  733.7 13.6 convolution_bitcast_fusion
  747.6 7.3 fusion.59
  755.7 7.9 fusion.63
  763.7 7.1 fusion.56
  771.5 16.6 fusion.64
  788.5 16.3 fusion.84
  810.0 4.6 convolution_bitcast_fusion.2
  814.7 4.6 convert_reduce_fusion.1
  819.9 41.6 %all-reduce.12 = (f32[6,1024]{1,0:T(8,128)S(1)}, bf16[1024]{0:T(1024)(128)(2,1)S(1)}, f32[4096]{0:T(1024)}, f32[3,1024]{1,0:T(4,128)}, f32[3,1024]{1,0:T(4,128)}) all-reduce(f32[6,1024]{1,0:T(8,128)S(1)} %stack.51, f32[1024]{0:T(1024)S(1)} %convert_reduce_fusion.6, f32[4096]{0:T(1024)S(1)} %copy-done.60, ...), channel_id=1, replica_groups=mesh['dp'=8,'mem'=4] {'dp'}, use_global_device_ids=true, to_apply=%region_35.36 | all-reduce | flops 17408 | bytes 137216 | tf_op jit(solution)/shard_map/psum | solution.py:277
  861.5 12.4 add_bitcast_fusion
  874.0 5.5 copy.85
  879.5 6.1 psum.68
  888.4 91.6 %reduce-scatter.8.cloned.1.call-done = f32[128,3072]{0,1:T(8,128)} async-done(((f32[1024,3072]{0,1:T(8,128)}), f32[128,3072]{0,1:T(8,128)}) %reduce-scatter.8.cloned.1.call-update) | async-done | bytes 1572880 | tf_op jit(solution)/shard_map/reduce_scatter | solution.py:269
  983.0 88.5 %reduce-scatter.16.cloned.1.call-done = f32[128,1024]{1,0:T(8,128)} async-done(((f32[1024,1024]{1,0:T(8,128)}), f32[128,1024]{1,0:T(8,128)}) %reduce-scatter.16.cloned.1.call-update) | async-done | bytes 524304 | tf_op jit(solution)/shard_map/reduce_scatter | solution.py:273
  1071.5 92.2 %reduce-scatter.12.cloned.1.call-done = f32[128,1024]{1,0:T(8,128)} async-done(((f32[1024,1024]{1,0:T(8,128)}), f32[128,1024]{1,0:T(8,128)}) %reduce-scatter.12.cloned.1.call-update) | async-done | bytes 524304 | tf_op jit(solution)/shard_map/reduce_scatter | solution.py:271
  1163.6 92.2 %reduce-scatter.10.cloned.1.call-done = f32[128,1024]{1,0:T(8,128)} async-done(((f32[1024,1024]{1,0:T(8,128)}), f32[128,1024]{1,0:T(8,128)}) %reduce-scatter.10.cloned.1.call-update) | async-done | bytes 524304 | tf_op jit(solution)/shard_map/reduce_scatter | solution.py:270
  1255.8 284.3 %reduce-scatter.18.cloned.1.call-done = f32[128,4096]{1,0:T(8,128)} async-done(((f32[1024,4096]{1,0:T(8,128)}), f32[128,4096]{1,0:T(8,128)}) %reduce-scatter.18.cloned.1.call-update) | async-done | bytes 2097168 | tf_op jit(solution)/shard_map/reduce_scatter | solution.py:274
  1540.2 283.6 %reduce-scatter.20.cloned.1.call-done = f32[512,1024]{1,0:T(8,128)} async-done(((f32[4096,1024]{1,0:T(8,128)}), f32[512,1024]{1,0:T(8,128)}) %reduce-scatter.20.cloned.1.call-update) | async-done | bytes 2097168 | tf_op jit(solution)/shard_map/reduce_scatter | solution.py:275
  (260 shorter events, 98.9 us)
Async XLA Ops:
  7.2 112.9 %copy-start = (bf16[1024,1024]{1,0:T(8,128)(2,1)S(1)}, bf16[1024,1024]{1,0:T(8,128)(2,1)}, u32[]{:S(2)}) copy-start(bf16[1024,1024]{1,0:T(8,128)(2,1)} %param.25) | copy-start | bytes 6291460
  7.2 443.1 %all-reduce.7.cloned.1.call-start = ((), (), s32[]{:S(2)}) async-start(), calls=%async_computation.7 | async-start | bytes 131072 | tf_op jit(solution)/shard_map/psum | solution.py:202
  8.7 10.3 copy-start.61
  89.6 24.3 %copy-start.34 = (f32[16,1024]{1,0:T(8,128)}, f32[16,1024]{1,0:T(8,128)S(1)}, u32[]{:S(2)}) copy-start(f32[16,1024]{1,0:T(8,128)S(1)} %get-tuple-element.238) | copy-start | bytes 196612
  89.6 24.3 %copy-start.28 = (bf16[1,1024,1024]{1,2,0:T(8,128)(2,1)S(1)}, bf16[1,1024,1024]{1,2,0:T(8,128)(2,1)}, u32[]{:S(2)}) copy-start(bf16[1,1024,1024]{1,2,0:T(8,128)(2,1)} %copy.62) | copy-start | bytes 6291460
  89.6 24.3 %copy-start.68 = (f32[1,1024]{1,0:T(1,128)S(1)}, f32[1,1024]{1,0:T(1,128)}, u32[]{:S(2)}) copy-start(f32[1,1024]{1,0:T(1,128)} %get-tuple-element.224) | copy-start | bytes 12292
  89.6 24.3 %copy-start.77 = (bf16[1024,1024]{1,0:T(8,128)(2,1)S(1)}, bf16[1024,1024]{1,0:T(8,128)(2,1)}, u32[]{:S(2)}) copy-start(bf16[1024,1024]{1,0:T(8,128)(2,1)} %param.24) | copy-start | bytes 6291460
  118.2 157.7 %copy-start.43 = (f32[1024]{0:T(1024)}, f32[1024]{0:T(1024)S(1)}, u32[]{:S(2)}) copy-start(f32[1024]{0:T(1024)S(1)} %broadcast_multiply_fusion.8) | copy-start | bytes 12292
  118.7 157.3 %copy-start.51 = (f32[1024]{0:T(1024)}, f32[1024]{0:T(1024)S(1)}, u32[]{:S(2)}) copy-start(f32[1024]{0:T(1024)S(1)} %add_rsqrt_fusion.2) | copy-start | bytes 12292
  128.2 32.0 %copy-start.63 = (pred[256]{0:T(512)(128)(4,1)}, pred[256]{0:T(512)(128)(4,1)S(1)}, u32[]{:S(2)}) copy-start(pred[256]{0:T(512)(128)(4,1)S(1)} %add_compare_fusion) | copy-start | bytes 772
  144.3 15.9 copy-start.32
  160.1 8.1 copy-start.19
  160.2 8.1 copy-start.21
  168.3 7.2 collective-permute-start
  178.5 93.1 %collective-permute-start.1 = (f32[1024,1024]{0,1:T(8,128)}, f32[1024,1024]{0,1:T(8,128)}, u32[]{:S(2)}, u32[]{:S(2)}) collective-permute-start(f32[1024,1024]{0,1:T(8,128)} %bitcast_add_fusion), channel_id=1, source_target_pairs={{0,2},{1,3},{2,0},{3,1},{4,6},{5,7},{6,4},{7,5},{8,10},{9,11},{10,... | collective-permute-start | bytes 12582920 | tf_op jit(solution)/shard_map/ppermute | solution.py:15
  184.0 92.0 %copy-start.9 = (f32[1024,1024]{0,1:T(8,128)S(1)}, f32[1024,1024]{0,1:T(8,128)}, u32[]{:S(2)}) copy-start(f32[1024,1024]{0,1:T(8,128)} %copy-done.8) | copy-start | bytes 12582916
  184.0 92.0 %copy-start.66 = (f32[1,1024]{1,0:T(1,128)S(1)}, f32[1,1024]{1,0:T(1,128)}, u32[]{:S(2)}) copy-start(f32[1,1024]{1,0:T(1,128)} %get-tuple-element.227) | copy-start | bytes 12292
  184.0 92.1 %copy-start.75 = (bf16[1024,1024]{1,0:T(8,128)(2,1)S(1)}, bf16[1024,1024]{1,0:T(8,128)(2,1)}, u32[]{:S(2)}) copy-start(bf16[1024,1024]{1,0:T(8,128)(2,1)} %param.27) | copy-start | bytes 6291460
  271.6 9.8 slice-start
  276.0 5.4 slice-start.1
  279.4 118.8 %copy-start.36 = (f32[1024]{0:T(1024)}, f32[1024]{0:T(1024)S(1)}, u32[]{:S(2)}) copy-start(f32[1024]{0:T(1024)S(1)} %broadcast_multiply_fusion.7) | copy-start | bytes 12292
  279.9 118.3 %copy-start.38 = (f32[1024]{0:T(1024)}, f32[1024]{0:T(1024)S(1)}, u32[]{:S(2)}) copy-start(f32[1024]{0:T(1024)S(1)} %add_rsqrt_fusion.1) | copy-start | bytes 12292
  281.4 46.4 %copy-start.65 = (f32[1,1024]{1,0:T(1,128)S(1)}, f32[1,1024]{1,0:T(1,128)}, u32[]{:S(2)}) copy-start(f32[1,1024]{1,0:T(1,128)} %get-tuple-element.221) | copy-start | bytes 12292
  327.8 19.7 %copy-start.6 = (bf16[1,1024,1024]{1,2,0:T(8,128)(2,1)S(1)}, bf16[1,1024,1024]{1,2,0:T(8,128)(2,1)}, u32[]{:S(2)}) copy-start(bf16[1,1024,1024]{1,2,0:T(8,128)(2,1)} %copy.73) | copy-start | bytes 6291460
  355.3 24.5 %copy-start.4 = (f32[1024,1024]{0,1:T(8,128)S(1)}, f32[1024,1024]{0,1:T(8,128)}, u32[]{:S(2)}) copy-start(f32[1024,1024]{0,1:T(8,128)} %copy-done.3) | copy-start | bytes 12582916
  402.7 14.6 copy-start.80
  417.4 140.8 %all-reduce.9.cloned.1.call-start = ((), (), s32[]{:S(2)}) async-start(), calls=%async_computation.8 | async-start | bytes 8388608 | tf_op jit(solution)/shard_map/psum | solution.py:207
  450.3 12.4 copy-start.15
  472.5 259.0 %reduce-scatter.14.cloned.1.call-start = ((), (), s32[]{:S(2)}) async-start(), calls=%async_computation.12 | async-start | bytes 9437184 | tf_op jit(solution)/shard_map/reduce_scatter | solution.py:272
  472.6 9.6 copy-start.7
  482.2 6.4 copy-start.24
  482.2 7.1 copy-start.31
  493.9 64.3 %copy-start.44 = (f32[1024]{0:T(1024)S(1)}, f32[1024]{0:T(1024)}, u32[]{:S(2)}) copy-start(f32[1024]{0:T(1024)} %copy-done.43) | copy-start | bytes 12292
  493.9 64.3 %copy-start.52 = (f32[1024]{0:T(1024)S(1)}, f32[1024]{0:T(1024)}, u32[]{:S(2)}) copy-start(f32[1024]{0:T(1024)} %copy-done.51) | copy-start | bytes 12292
  493.9 64.3 %copy-start.57 = (f32[1,1024]{1,0:T(1,128)S(1)}, f32[1,1024]{1,0:T(1,128)}, u32[]{:S(2)}) copy-start(f32[1,1024]{1,0:T(1,128)} %get-tuple-element.229) | copy-start | bytes 12292
  493.9 392.3 %all-reduce.11.cloned.1.call-start = ((), (), s32[]{:S(2)}) async-start(), calls=%async_computation.13 | async-start | bytes 1048576 | tf_op jit(solution)/shard_map/psum | solution.py:279
  558.2 8.5 copy-start.10
  571.1 44.3 %copy-start.81 = (bf16[1024,1024]{0,1:T(8,128)(2,1)}, bf16[1024,1024]{0,1:T(8,128)(2,1)S(1)}, u32[]{:S(2)}) copy-start(bf16[1024,1024]{0,1:T(8,128)(2,1)S(1)} %convolution_convert_fusion.1) | copy-start | bytes 6291460
  615.4 54.7 %copy-start.11 = (bf16[1024,1024]{0,1:T(8,128)(2,1)S(1)}, bf16[1024,1024]{0,1:T(8,128)(2,1)}, u32[]{:S(2)}) copy-start(bf16[1024,1024]{0,1:T(8,128)(2,1)} %copy.64) | copy-start | bytes 6291460
  706.2 27.5 %copy-start.12 = (bf16[16,64,1024]{2,1,0:T(8,128)(2,1)S(1)}, bf16[16,64,1024]{2,1,0:T(8,128)(2,1)}, u32[]{:S(2)}) copy-start(bf16[16,64,1024]{2,1,0:T(8,128)(2,1)} %convolution_convert_fusion) | copy-start | bytes 6291460
  733.7 246.3 %reduce-scatter.8.cloned.1.call-start = ((), (), s32[]{:S(2)}) async-start(), calls=%async_computation.9 | async-start | bytes 14155776 | tf_op jit(solution)/shard_map/reduce_scatter | solution.py:269
  747.4 324.1 %reduce-scatter.16.cloned.1.call-start = ((), (), s32[]{:S(2)}) async-start(), calls=%async_computation.14 | async-start | bytes 4718592 | tf_op jit(solution)/shard_map/reduce_scatter | solution.py:273
  755.0 408.7 %reduce-scatter.12.cloned.1.call-start = ((), (), s32[]{:S(2)}) async-start(), calls=%async_computation.11 | async-start | bytes 4718592 | tf_op jit(solution)/shard_map/reduce_scatter | solution.py:271
  763.6 492.2 %reduce-scatter.10.cloned.1.call-start = ((), (), s32[]{:S(2)}) async-start(), calls=%async_computation.10 | async-start | bytes 4718592 | tf_op jit(solution)/shard_map/reduce_scatter | solution.py:270
  770.9 769.3 %reduce-scatter.18.cloned.1.call-start = ((), (), s32[]{:S(2)}) async-start(), calls=%async_computation.15 | async-start | bytes 18874368 | tf_op jit(solution)/shard_map/reduce_scatter | solution.py:274
  788.2 1035.6 %reduce-scatter.20.cloned.1.call-start = ((), (), s32[]{:S(2)}) async-start(), calls=%async_computation.16 | async-start | bytes 18874368 | tf_op jit(solution)/shard_map/reduce_scatter | solution.py:275
  814.7 5.1 copy-start.60
  874.0 949.8 %copy-start.1 = (bf16[1024,1024]{1,0:T(8,128)(2,1)S(1)}, bf16[1024,1024]{1,0:T(8,128)(2,1)}, u32[]{:S(2)}) copy-start(bf16[1024,1024]{1,0:T(8,128)(2,1)} %param.25) | copy-start | bytes 6291460
  (48 other events, 134.6 us)
Sparse Core Ops, SparseCore 0:
  417.5 32.7 all-reduce.6
  472.7 85.4 all-reduce.8
  561.8 147.9 reduce-scatter.13
  733.8 33.1 all-reduce.10
  770.5 209.4 reduce-scatter.7
  984.0 87.3 reduce-scatter.15
  1075.7 87.9 reduce-scatter.11
  1167.8 87.9 reduce-scatter.9
  1260.2 279.9 reduce-scatter.17
  1544.4 279.3 reduce-scatter.19
